TPU v7x, 32 devices: a whole 2x2x4 slice. The times are simulated.
32 devices in a mesh: gx: 16 (over z, y, core), gy: 2 (over x).
Axes of the slice: x: 2, y: 2, z: 4, core: 2. Of those that a mesh axis runs over, the one named last changes fastest.
Arguments:
- inputs: bfloat16 [128, 8192], P('gy', 'gx'), may hold values from -6 to 6
- gate_pre: bfloat16 [128, 28672], P('gx', 'gy'), may hold values from -8 to 8
- up_pre: bfloat16 [128, 28672], P('gx', 'gy'), may hold values from -6 to 6
- out_grad: bfloat16 [128, 8192], P('gy', 'gx'), may hold values from -6 to 6
- w_gate: bfloat16 [8192, 28672], P('gx', 'gy'), may hold values from -0.0625 to 0.0625
- w_up: bfloat16 [8192, 28672], P('gx', 'gy'), may hold values from -0.0625 to 0.0625
- w_down: bfloat16 [28672, 8192], P('gy', 'gx'), may hold values from -0.03125 to 0.03125
Outputs:
- grad_input: bfloat16 [128, 8192], P('gy', 'gx')
- grad_w_gate: bfloat16 [8192, 28672], P('gx', 'gy')
- grad_w_up: bfloat16 [8192, 28672], P('gx', 'gy')
- grad_w_down: bfloat16 [28672, 8192], P('gy', 'gx')
All inputs are finite; a program needn't handle non-finite values.
Results may differ from a plain program's by a relative error of at most 0.017.
Values may be sent and summed in bfloat16 or wider, within the bound.
A program may use at most 256 MiB of HBM per device.

v0:
```python
import jax
import jax.numpy as jnp
from jax import lax
from jax.sharding import PartitionSpec as P


def swiglu_back(d_hidden, gate_pre, up_pre):
    gate_val = gate_pre.astype(jnp.float32)
    up_val = up_pre.astype(jnp.float32)
    sig = jax.nn.sigmoid(gate_val)
    silu_val = gate_val * sig
    hidden = (silu_val * up_val).astype(jnp.bfloat16)
    d_up = (d_hidden * silu_val).astype(jnp.bfloat16)
    d_gate = (d_hidden * up_val * sig * (1.0 + gate_val * (1.0 - sig))).astype(jnp.bfloat16)
    return (d_gate, d_up, hidden)


def contract_rows(left, right):
    return lax.dot_general(
        left, right, (((0,), (0,)), ((), ())), preferred_element_type=jnp.float32
    )


def contract_cols(left, right):
    return lax.dot_general(
        left, right, (((1,), (1,)), ((), ())), preferred_element_type=jnp.float32
    )


def per_device(inputs, gate_pre, up_pre, out_grad, w_gate, w_up, w_down):
    input_rows, grad_rows = (
        lax.all_gather(inputs, "gy", axis=0, tiled=True),
        lax.all_gather(out_grad, "gy", axis=0, tiled=True),
    )
    d_hidden = lax.psum_scatter(
        contract_cols(grad_rows, w_down).astype(jnp.bfloat16), "gx", scatter_dimension=0, tiled=True
    ).astype(jnp.float32)
    d_gate, d_up, hidden = swiglu_back(d_hidden, gate_pre, up_pre)
    gate_piece = lax.all_gather(d_gate, "gx", axis=0, tiled=True)
    up_piece = lax.all_gather(d_up, "gx", axis=0, tiled=True)
    hidden_piece = lax.all_gather(hidden, "gx", axis=0, tiled=True)
    gate_total = contract_rows(input_rows, gate_piece)
    up_total = contract_rows(input_rows, up_piece)
    down_total = contract_rows(hidden_piece, grad_rows)
    input_block_grad = contract_cols(gate_piece, w_gate) + contract_cols(up_piece, w_up)
    input_total = input_block_grad
    gate_total, up_total, down_total, input_total = (gate_total, up_total, down_total, input_total)
    grad_input = lax.psum_scatter(
        input_total.astype(jnp.bfloat16), "gy", scatter_dimension=0, tiled=True
    )
    return (
        grad_input,
        gate_total.astype(jnp.bfloat16),
        up_total.astype(jnp.bfloat16),
        down_total.astype(jnp.bfloat16),
    )


def solution(mesh):
    placed = (
        P("gy", "gx"),
        P("gx", "gy"),
        P("gx", "gy"),
        P("gy", "gx"),
        P("gx", "gy"),
        P("gx", "gy"),
        P("gy", "gx"),
    )
    return jax.shard_map(
        per_device,
        mesh=mesh,
        in_specs=placed,
        out_specs=(P("gy", "gx"), P("gx", "gy"), P("gx", "gy"), P("gy", "gx")),
        check_vma=False,
    )
```

profile of v0, /device:TPU:0, one launch (start us, length us, event | category | flops | bytes accessed | tf_op | source)
XLA Modules:
  0.0 300.6 jit_solution(5242010842057136992)
XLA Ops:
  7.2 0.0 copy-start.2
  7.2 0.0 copy-start.1
  7.2 0.0 copy-start.3
  7.2 0.0 reduce-scatter.3.cloned.1.call-start
  7.2 6.2 %all_gather.15 = bf16[128,512]{1,0:T(8,128)(2,1)S(1)} all-gather(bf16[64,512]{1,0:T(8,128)(2,1)} %param.10), channel_id=1, replica_groups=mesh['gx'=16,'gy'=2] {'gy'}, dimensions={0}, use_global_device_ids=true | all-gather | bytes 196608 | tf_op jit(solution)/shard_map/all_gather | solution.py:33
  13.5 11.8 %convolution_convert_fusion.3 = bf16[128,14336]{1,0:T(8,128)(2,1)} fusion(bf16[128,512]{1,0:T(8,128)(2,1)S(1)} %all_gather.15, bf16[14336,512]{1,0:T(8,128)(2,1)} %param.13), kind=kOutput, calls=%fused_computation.5 | convolution fusion | flops 1880883200 | bytes 18481152 | tf_op jit(solution)/shard_map/dot_general | solution.py:25
  25.3 0.0 reduce-scatter.3.cloned.1.call-update
  25.3 0.0 all-gather.4.cloned.1.call-start
  25.4 70.5 %reduce-scatter.3.cloned.1.call-done = bf16[8,14336]{1,0:T(8,128)(2,1)} async-done(((bf16[128,14336]{1,0:T(8,128)(2,1)}), bf16[8,14336]{1,0:T(8,128)(2,1)}) %reduce-scatter.3.cloned.1.call-update) | async-done | bytes 229392 | tf_op jit(solution)/shard_map/reduce_scatter | solution.py:35
  95.9 0.0 copy-done.2
  95.9 0.0 copy-done.1
  95.9 2.0 fusion.7
  97.9 0.0 all-gather.4.cloned.1.call-update
  97.9 0.0 all-gather.6.cloned.1.call-start
  98.0 0.7 all-gather.6.cloned.1.call-update
  98.7 0.0 all-gather.8.cloned.1.call-start
  98.7 0.5 all-gather.8.cloned.1.call-update
  99.2 0.0 reduce-scatter.5.cloned.1.call-start
  99.3 0.0 copy-done.3
  99.3 4.9 %all_gather.18 = bf16[128,512]{1,0:T(8,128)(2,1)S(1)} all-gather(bf16[64,512]{1,0:T(8,128)(2,1)S(1)} %copy-done.3), channel_id=1, replica_groups=mesh['gx'=16,'gy'=2] {'gy'}, dimensions={0}, use_global_device_ids=true | all-gather | bytes 196608 | tf_op jit(solution)/shard_map/all_gather | solution.py:32
  104.2 41.1 %all-gather.4.cloned.1.call-done = bf16[128,14336]{1,0:T(8,128)(2,1)} async-done(((bf16[8,14336]{1,0:T(8,128)(2,1)}), bf16[128,14336]{1,0:T(8,128)(2,1)}) %all-gather.4.cloned.1.call-update) | async-done | bytes 3670032 | tf_op jit(solution)/shard_map/all_gather | solution.py:39
  145.4 11.3 %fusion.12 = f32[128,512]{1,0:T(8,128)S(1)} fusion(bf16[128,14336]{1,0:T(8,128)(2,1)} %all-gather.4.cloned.1.call-done, bf16[512,14336]{1,0:T(8,128)(2,1)} %param.11), kind=kOutput, calls=%fused_computation.23 | convolution fusion | flops 1879048192 | bytes 18612224 | tf_op jit(solution)/shard_map/dot_general | solution.py:25
  156.7 38.4 %all-gather.6.cloned.1.call-done = bf16[128,14336]{1,0:T(8,128)(2,1)} async-done(((bf16[8,14336]{1,0:T(8,128)(2,1)}), bf16[128,14336]{1,0:T(8,128)(2,1)}) %all-gather.6.cloned.1.call-update) | async-done | bytes 3670032 | tf_op jit(solution)/shard_map/all_gather | solution.py:40
  195.1 11.9 %fusion.2 = bf16[128,512]{1,0:T(8,128)(2,1)} fusion(f32[128,512]{1,0:T(8,128)S(1)} %fusion.12, bf16[128,14336]{1,0:T(8,128)(2,1)} %all-gather.6.cloned.1.call-done, bf16[512,14336]{1,0:T(8,128)(2,1)} %param.12), kind=kOutput, calls=%fused_computation.7 | convolution fusion | flops 1879179264 | bytes 18743296 | tf_op jit(solution)/shard_map/dot_general | solution.py:25
  207.1 0.0 reduce-scatter.5.cloned.1.call-update
  207.1 0.0 copy-start
  207.1 10.0 %fusion = bf16[512,14336]{0,1:T(8,128)(2,1)} fusion(bf16[128,14336]{1,0:T(8,128)(2,1)} %all-gather.4.cloned.1.call-done, bf16[128,512]{1,0:T(8,128)(2,1)S(1)} %all_gather.18), kind=kOutput, calls=%fused_computation.3 | convolution fusion | flops 1886388224 | bytes 18481152 | tf_op jit(solution)/shard_map/dot_general | solution.py:19
  217.0 7.5 %fusion.1 = bf16[512,14336]{0,1:T(8,128)(2,1)} fusion(bf16[128,14336]{1,0:T(8,128)(2,1)S(1)} %copy-done, bf16[128,512]{1,0:T(8,128)(2,1)S(1)} %all_gather.18), kind=kOutput, calls=%fused_computation.4 | convolution fusion | flops 1886388224 | bytes 18481152 | tf_op jit(solution)/shard_map/dot_general | solution.py:19
  224.6 20.1 %all-gather.8.cloned.1.call-done = bf16[128,14336]{1,0:T(8,128)(2,1)} async-done(((bf16[8,14336]{1,0:T(8,128)(2,1)}), bf16[128,14336]{1,0:T(8,128)(2,1)}) %all-gather.8.cloned.1.call-update) | async-done | bytes 3670032 | tf_op jit(solution)/shard_map/all_gather | solution.py:41
  244.7 9.6 %convolution_convert_fusion = bf16[14336,512]{1,0:T(8,128)(2,1)} fusion(bf16[128,14336]{1,0:T(8,128)(2,1)} %all-gather.8.cloned.1.call-done, bf16[128,512]{1,0:T(8,128)(2,1)S(1)} %all_gather.15), kind=kOutput, calls=%fused_computation | convolution fusion | flops 1886388224 | bytes 18481152 | tf_op jit(solution)/shard_map/dot_general | solution.py:19
  254.3 19.9 %copy.11 = bf16[512,14336]{1,0:T(8,128)(2,1)} copy(bf16[512,14336]{0,1:T(8,128)(2,1)} %fusion) | data formatting | bytes 29360128
  274.2 19.9 %copy.12 = bf16[512,14336]{1,0:T(8,128)(2,1)} copy(bf16[512,14336]{0,1:T(8,128)(2,1)} %fusion.1) | data formatting | bytes 29360128
  (2 shorter events, 0.0 us)
Async XLA Ops:
  7.2 88.7 %copy-start.2 = (bf16[8,14336]{1,0:T(8,128)(2,1)S(1)}, bf16[8,14336]{1,0:T(8,128)(2,1)}, u32[]{:S(2)}) copy-start(bf16[8,14336]{1,0:T(8,128)(2,1)} %param.8) | copy-start | bytes 688132
  7.2 88.7 %copy-start.1 = (bf16[8,14336]{1,0:T(8,128)(2,1)S(1)}, bf16[8,14336]{1,0:T(8,128)(2,1)}, u32[]{:S(2)}) copy-start(bf16[8,14336]{1,0:T(8,128)(2,1)} %param.9) | copy-start | bytes 688132
  7.2 92.1 %copy-start.3 = (bf16[64,512]{1,0:T(8,128)(2,1)S(1)}, bf16[64,512]{1,0:T(8,128)(2,1)}, u32[]{:S(2)}) copy-start(bf16[64,512]{1,0:T(8,128)(2,1)} %param.7) | copy-start | bytes 196612
  7.2 88.7 %reduce-scatter.3.cloned.1.call-start = ((), (), s32[]{:S(2)}) async-start(), calls=%async_computation.2 | async-start | bytes 3899392 | tf_op jit(solution)/shard_map/reduce_scatter | solution.py:35
  25.3 120.0 %all-gather.4.cloned.1.call-start = ((), (), s32[]{:S(2)}) async-start(), calls=%async_computation.3 | async-start | bytes 3899392 | tf_op jit(solution)/shard_map/all_gather | solution.py:39
  97.9 97.2 %all-gather.6.cloned.1.call-start = ((), (), s32[]{:S(2)}) async-start(), calls=%async_computation.4 | async-start | bytes 3899392 | tf_op jit(solution)/shard_map/all_gather | solution.py:40
  98.7 146.0 %all-gather.8.cloned.1.call-start = ((), (), s32[]{:S(2)}) async-start(), calls=%async_computation.6 | async-start | bytes 3899392 | tf_op jit(solution)/shard_map/all_gather | solution.py:41
  99.2 194.9 %reduce-scatter.5.cloned.1.call-start = ((), (), s32[]{:S(2)}) async-start(), calls=%async_computation.5 | async-start | bytes 196608 | tf_op jit(solution)/shard_map/reduce_scatter | solution.py:48
  207.1 10.0 %copy-start = (bf16[128,14336]{1,0:T(8,128)(2,1)S(1)}, bf16[128,14336]{1,0:T(8,128)(2,1)}, u32[]{:S(2)}) copy-start(bf16[128,14336]{1,0:T(8,128)(2,1)} %all-gather.6.cloned.1.call-done) | copy-start | bytes 11010052
Sparse Core Ops, SparseCore 0:
  25.5 70.3 reduce-scatter.2
  99.0 46.3 all-gather.3
  148.5 46.5 all-gather.5
  198.1 46.5 all-gather.7
  247.4 9.2 reduce-scatter.4
where the time goes:
time: 302 us; the launch traced here: 301 us
  waiting for transfers between devices  171 us (57%)
  matrix products  62.2 us (21%)
  local copies, waits for them, and re-layouts  39.8 us (13%)
  between operations  13.8 us (5%)
  blocking collectives  11.2 us (4%)
    reduce_scatter x1, waiting for transfers between devices, per_device(): lax.psum_scatter(contract_cols(grad_rows, w_down).astype(jnp.bfloat16), '...  70.5 us
    all_gather x1, waiting for transfers between devices, per_device(): gate_piece = lax.all_gather(d_gate, 'gx', axis=0, tiled=True)  41.1 us
    unnamed x10, local copies, waits for them, and re-layouts  39.8 us
    all_gather x1, waiting for transfers between devices, per_device(): up_piece = lax.all_gather(d_up, 'gx', axis=0, tiled=True)  38.4 us
    dot_general x3, matrix products, contract_cols(): lax.dot_general(left, right, (((1,), (1,)), ((), ())), preferred_element_...  35.1 us
    dot_general x3, matrix products, contract_rows(): lax.dot_general(left, right, (((0,), (0,)), ((), ())), preferred_element_...  27.1 us
    all_gather x1, waiting for transfers between devices, per_device(): hidden_piece = lax.all_gather(hidden, 'gx', axis=0, tiled=True)  20.1 us
    all_gather x1, blocking collectives, per_device(): lax.all_gather(out_grad, 'gy', axis=0, tiled=True)  6.24 us
  transfers between devices with their start and end apart: 5, of which 4 were waited for; matrix products, arithmetic and copies ran while one was open for 30% of the time, Pallas kernels for 0%

commit v1 on v0

--- a/solution.py
+++ b/solution.py
@@ -37,8 +37,11 @@
     ).astype(jnp.float32)
     d_gate, d_up, hidden = swiglu_back(d_hidden, gate_pre, up_pre)
     gate_piece = lax.all_gather(d_gate, "gx", axis=0, tiled=True)
-    up_piece = lax.all_gather(d_up, "gx", axis=0, tiled=True)
-    hidden_piece = lax.all_gather(hidden, "gx", axis=0, tiled=True)
+    up_piece, hidden_piece = jnp.split(
+        jax.lax.all_gather(jnp.concatenate([d_up, hidden], 1), axis_name="gx", axis=0, tiled=True),
+        [d_up.shape[1]],
+        1,
+    )
     gate_total = contract_rows(input_rows, gate_piece)
     up_total = contract_rows(input_rows, up_piece)
     down_total = contract_rows(hidden_piece, grad_rows)

time: 302 us -> 275 us (0.911)
  waiting for transfers between devices: 171 us -> 141 us
    all_gather x2 -> x1, waiting for transfers between devices: 58.5 us -> 28.7 us  [per_device(): jax.lax.all_gather(jnp.concatenate([d_up, hidden], 1), axis_name='gx', ax...]
    unnamed x10 -> x8, local copies, waits for them, and re-layouts: 39.8 us -> 39.9 us
  transfers between devices with their start and end apart: 5 -> 4, of which waited for: 4 -> 3; matrix products, arithmetic and copies ran while one was open for 30% -> 30% of each run, Pallas kernels for 0% -> 0%
where the time goes in v1:
time: 275 us; the launch traced here: 273 us
  waiting for transfers between devices  141 us (51%)
  matrix products  64.6 us (23%)
  local copies, waits for them, and re-layouts  39.9 us (15%)
  between operations  13.8 us (5%)
  blocking collectives  11.4 us (4%)
    reduce_scatter x1, waiting for transfers between devices, per_device(): lax.psum_scatter(contract_cols(grad_rows, w_down).astype(jnp.bfloat16), '...  70.5 us
    all_gather x1, waiting for transfers between devices, per_device(): gate_piece = lax.all_gather(d_gate, 'gx', axis=0, tiled=True)  41.5 us
    unnamed x8, local copies, waits for them, and re-layouts  39.9 us
    dot_general x3, matrix products, contract_cols(): lax.dot_general(left, right, (((1,), (1,)), ((), ())), preferred_element_...  36 us
    all_gather x1, waiting for transfers between devices, per_device(): jax.lax.all_gather(jnp.concatenate([d_up, hidden], 1), axis_name='gx', ax...  28.7 us
    dot_general x3, matrix products, contract_rows(): lax.dot_general(left, right, (((0,), (0,)), ((), ())), preferred_element_...  28.6 us
    all_gather x1, blocking collectives, per_device(): lax.all_gather(out_grad, 'gy', axis=0, tiled=True)  6.24 us
  transfers between devices with their start and end apart: 4, of which 3 were waited for; matrix products, arithmetic and copies ran while one was open for 30% of the time, Pallas kernels for 0%

profile of v1, /device:TPU:0, one launch (start us, length us, event | category | flops | bytes accessed | tf_op | source)
XLA Modules:
  0.0 273.3 jit_solution(8901802857804301096)
XLA Ops:
  7.2 0.0 copy-start.1
  7.2 0.0 copy-start
  7.2 0.0 copy-start.2
  7.2 0.0 reduce-scatter.3.cloned.1.call-start
  7.2 6.2 %all_gather.12 = bf16[128,512]{1,0:T(8,128)(2,1)S(1)} all-gather(bf16[64,512]{1,0:T(8,128)(2,1)} %param.10), channel_id=1, replica_groups=mesh['gx'=16,'gy'=2] {'gy'}, dimensions={0}, use_global_device_ids=true | all-gather | bytes 196608 | tf_op jit(solution)/shard_map/all_gather | solution.py:33
  13.5 11.8 %convolution_convert_fusion.3 = bf16[128,14336]{1,0:T(8,128)(2,1)} fusion(bf16[128,512]{1,0:T(8,128)(2,1)S(1)} %all_gather.12, bf16[14336,512]{1,0:T(8,128)(2,1)} %param.13), kind=kOutput, calls=%fused_computation.5 | convolution fusion | flops 1880883200 | bytes 18481152 | tf_op jit(solution)/shard_map/dot_general | solution.py:25
  25.3 0.0 reduce-scatter.3.cloned.1.call-update
  25.3 0.0 all-gather.3.cloned.1.call-start
  25.4 70.5 %reduce-scatter.3.cloned.1.call-done = bf16[8,14336]{1,0:T(8,128)(2,1)} async-done(((bf16[128,14336]{1,0:T(8,128)(2,1)}), bf16[8,14336]{1,0:T(8,128)(2,1)}) %reduce-scatter.3.cloned.1.call-update) | async-done | bytes 229392 | tf_op jit(solution)/shard_map/reduce_scatter | solution.py:35
  95.9 0.0 copy-done.1
  95.9 0.0 copy-done
  95.9 1.9 fusion.12
  97.8 0.0 all-gather.3.cloned.1.call-update
  97.8 0.0 all-gather.5.cloned.1.call-start
  97.8 0.8 pad_maximum_fusion
  98.6 0.0 all-gather.5.cloned.1.call-update
  98.7 0.0 reduce-scatter.5.cloned.1.call-start
  98.7 0.0 copy-done.2
  98.7 5.1 %all_gather.15 = bf16[128,512]{1,0:T(8,128)(2,1)S(1)} all-gather(bf16[64,512]{1,0:T(8,128)(2,1)S(1)} %copy-done.2), channel_id=1, replica_groups=mesh['gx'=16,'gy'=2] {'gy'}, dimensions={0}, use_global_device_ids=true | all-gather | bytes 196608 | tf_op jit(solution)/shard_map/all_gather | solution.py:32
  103.9 41.5 %all-gather.3.cloned.1.call-done = bf16[128,14336]{1,0:T(8,128)(2,1)} async-done(((bf16[8,14336]{1,0:T(8,128)(2,1)}), bf16[128,14336]{1,0:T(8,128)(2,1)}) %all-gather.3.cloned.1.call-update) | async-done | bytes 3670032 | tf_op jit(solution)/shard_map/all_gather | solution.py:39
  145.4 9.6 %fusion = bf16[512,14336]{0,1:T(8,128)(2,1)} fusion(bf16[128,14336]{1,0:T(8,128)(2,1)} %all-gather.3.cloned.1.call-done, bf16[128,512]{1,0:T(8,128)(2,1)S(1)} %all_gather.15), kind=kOutput, calls=%fused_computation.3 | convolution fusion | flops 1886388224 | bytes 18481152 | tf_op jit(solution)/shard_map/dot_general | solution.py:19
  155.0 20.0 %copy.11 = bf16[512,14336]{1,0:T(8,128)(2,1)} copy(bf16[512,14336]{0,1:T(8,128)(2,1)} %fusion) | data formatting | bytes 29360128
  174.9 12.2 %fusion.21 = f32[128,512]{1,0:T(8,128)S(1)} fusion(bf16[128,14336]{1,0:T(8,128)(2,1)} %all-gather.3.cloned.1.call-done, bf16[512,14336]{1,0:T(8,128)(2,1)} %param.11), kind=kOutput, calls=%fused_computation.28 | convolution fusion | flops 1879048192 | bytes 18612224 | tf_op jit(solution)/shard_map/dot_general | solution.py:25
  187.2 28.7 %all-gather.5.cloned.1.call-done = bf16[128,28672]{1,0:T(8,128)(2,1)} async-done(((bf16[8,28672]{1,0:T(8,128)(2,1)}), bf16[128,28672]{1,0:T(8,128)(2,1)}) %all-gather.5.cloned.1.call-update) | async-done | bytes 7340048 | tf_op jit(solution)/shard_map/all_gather | solution.py:41
  215.8 12.0 %fusion.9 = bf16[128,512]{1,0:T(8,128)(2,1)} fusion(f32[128,512]{1,0:T(8,128)S(1)} %fusion.21, bf16[512,14336]{1,0:T(8,128)(2,1)} %param.12, bf16[128,28672]{1,0:T(8,128)(2,1)} %all-gather.5.cloned.1.call-done), kind=kOutput, calls=%fused_computation.11 | convolution fusion | flops 1879179264 | bytes 18743296 | tf_op jit(solution)/shard_map/dot_general | solution.py:25
  227.8 0.0 reduce-scatter.5.cloned.1.call-update
  227.8 9.4 %fusion.1 = bf16[512,14336]{0,1:T(8,128)(2,1)} fusion(bf16[128,512]{1,0:T(8,128)(2,1)S(1)} %all_gather.15, bf16[128,28672]{1,0:T(8,128)(2,1)} %all-gather.5.cloned.1.call-done), kind=kOutput, calls=%fused_computation.4 | convolution fusion | flops 1886388224 | bytes 18481152 | tf_op jit(solution)/shard_map/dot_general | solution.py:19
  237.2 9.6 %convolution_convert_fusion = bf16[14336,512]{1,0:T(8,128)(2,1)} fusion(bf16[128,512]{1,0:T(8,128)(2,1)S(1)} %all_gather.12, bf16[128,28672]{1,0:T(8,128)(2,1)} %all-gather.5.cloned.1.call-done), kind=kOutput, calls=%fused_computation | convolution fusion | flops 1886388224 | bytes 18481152 | tf_op jit(solution)/shard_map/dot_general | solution.py:19
  246.8 19.9 %copy.12 = bf16[512,14336]{1,0:T(8,128)(2,1)} copy(bf16[512,14336]{0,1:T(8,128)(2,1)} %fusion.1) | data formatting | bytes 29360128
  266.7 0.0 reduce-scatter.5.cloned.1.call-done
Async XLA Ops:
  7.2 88.7 %copy-start.1 = (bf16[8,14336]{1,0:T(8,128)(2,1)S(1)}, bf16[8,14336]{1,0:T(8,128)(2,1)}, u32[]{:S(2)}) copy-start(bf16[8,14336]{1,0:T(8,128)(2,1)} %param.9) | copy-start | bytes 688132
  7.2 88.7 %copy-start = (bf16[8,14336]{1,0:T(8,128)(2,1)S(1)}, bf16[8,14336]{1,0:T(8,128)(2,1)}, u32[]{:S(2)}) copy-start(bf16[8,14336]{1,0:T(8,128)(2,1)} %param.8) | copy-start | bytes 688132
  7.2 91.5 %copy-start.2 = (bf16[64,512]{1,0:T(8,128)(2,1)S(1)}, bf16[64,512]{1,0:T(8,128)(2,1)}, u32[]{:S(2)}) copy-start(bf16[64,512]{1,0:T(8,128)(2,1)} %param.7) | copy-start | bytes 196612
  7.2 88.7 %reduce-scatter.3.cloned.1.call-start = ((), (), s32[]{:S(2)}) async-start(), calls=%async_computation.2 | async-start | bytes 3899392 | tf_op jit(solution)/shard_map/reduce_scatter | solution.py:35
  25.3 120.0 %all-gather.3.cloned.1.call-start = ((), (), s32[]{:S(2)}) async-start(), calls=%async_computation.3 | async-start | bytes 3899392 | tf_op jit(solution)/shard_map/all_gather | solution.py:39
  97.8 118.0 %all-gather.5.cloned.1.call-start = ((), (), s32[]{:S(2)}) async-start(), calls=%async_computation.4 | async-start | bytes 7798784 | tf_op jit(solution)/shard_map/all_gather | solution.py:41
  98.7 168.1 %reduce-scatter.5.cloned.1.call-start = ((), (), s32[]{:S(2)}) async-start(), calls=%async_computation.5 | async-start | bytes 196608 | tf_op jit(solution)/shard_map/reduce_scatter | solution.py:51
Sparse Core Ops, SparseCore 0:
  25.5 70.3 reduce-scatter.2
  99.0 46.3 all-gather.2
  148.5 67.3 all-gather.4
  227.9 8.6 reduce-scatter.4
